TPU v7x, 32 devices: a whole 2x2x4 slice. The times are simulated.
32 devices in a mesh: wide: 16 (over z, y, x), narrow: 2 (over core).
Axes of the slice: x: 2, y: 2, z: 4, core: 2. Of those that a mesh axis runs over, the one named last changes fastest.
Arguments:
- blocks: float32 [256, 14, 128, 128], P('wide', 'narrow'), may hold values from -0.125 to 0.125
- vectors: float32 [32768, 512], P('wide'), may hold values from -1.5 to 1.5
- sign_bits: int32 [32768], P('wide'), may hold values from 0 to 1
- column_blocks: int32 [256, 14], P('wide', 'narrow'), may hold values from 0 to 255, as said below
- sample_rows: int32 [1024], P('wide'), may hold values from 0 to 32767, as said below
Outputs:
- sketch: float32 [1024, 512], P('wide', 'narrow')
Inputs may be any that keep to these rules, and one draw needn't show every extreme that they name: `column_blocks`: entry [g, j] equals (g + o) mod 256 for an offset o with -8 <= o <= 8; both offsets -8 and 8 occur in every draw. `sample_rows`: entries 64 * w to 64 * w + 63 are distinct rows of slab w, that is of rows 16 * 128 * w to 16 * 128 * w + 16 * 128 - 1, in increasing order.
All inputs are finite; a program needn't handle non-finite values.
Results may differ from a plain program's by a relative error of at most 0.00013.
Values sent between devices are 32-bit elements; how exact they have to be, the bound alone decides.
A program may use at most 192 MiB of HBM per device.

v0:
```python
import math

import jax
import jax.numpy as jnp
from jax import lax
from jax.sharding import PartitionSpec as P

REACH = 8


def extended_2(array, sides, width):
    for axis, dim in sides:
        size, length = (lax.axis_size(axis), array.shape[dim])
        up = [(i, (i + 1) % size) for i in range(size)]
        down = [(j, i) for i, j in up]
        last = lax.slice_in_dim(array, length - width, length, axis=dim)
        initial = lax.slice_in_dim(array, 0, width, axis=dim)
        before = lax.ppermute(last, axis, up)
        after = lax.ppermute(initial, axis, down)
        array = jnp.concatenate([before, array, after], axis=dim)
    return array


def sylvester_matrix(order):
    positions = jnp.arange(order, dtype=jnp.int32)
    common = positions[:, None] & positions[None, :]
    parity = jnp.zeros((order, order), jnp.int32)
    for shift_bits in range(max(order - 1, 1).bit_length()):
        parity = parity + (common >> shift_bits & 1)
    return (1 - 2 * (parity % 2)).astype(jnp.float32)


def local(blocks, vectors, sign_bits, column_blocks, sample_rows):
    highest = lax.Precision.HIGHEST
    slab_rows = blocks.shape[0]
    slot_count = blocks.shape[1]
    order = blocks.shape[2]
    width = vectors.shape[1]
    wide_count = lax.axis_size("wide")
    half_width = width // lax.axis_size("narrow")
    extended = extended_2(vectors, (("wide", 0),), REACH * order)
    ext_blocks = extended.reshape(slab_rows + 2 * REACH, order, width)
    total_blocks = slab_rows * wide_count
    slab_index = lax.axis_index("wide")
    local_columns = (column_blocks - slab_index * slab_rows + REACH) % total_blocks
    running = jnp.zeros((half_width * lax.axis_size("narrow"), slab_rows, order), jnp.float32)
    for slot_number in range(slot_count):
        picked = jnp.take(ext_blocks, local_columns[:, slot_number], axis=0)
        running = running + jnp.einsum(
            "bik,bkn->nbi", blocks[:, slot_number], picked, precision=highest
        )
    product = lax.psum_scatter(
        running.reshape(half_width * lax.axis_size("narrow"), slab_rows * order),
        "narrow",
        scatter_dimension=0,
        tiled=True,
    )
    signs = (2 * sign_bits - 1).astype(jnp.float32)
    signed = (product * signs[None, :]).reshape(half_width, slab_rows, order)
    mixed = jnp.einsum("nbk,ik->nbi", signed, sylvester_matrix(order), precision=highest)
    mixed = mixed.reshape(half_width, slab_rows * order)
    samples_slab = sample_rows.shape[0]
    slab_total = slab_rows * order
    scale = math.sqrt(slab_total * wide_count / (samples_slab * wide_count)) / math.sqrt(
        order * wide_count
    )
    wide_matrix = sylvester_matrix(wide_count)
    all_samples = lax.all_gather(sample_rows, "wide", axis=0, tiled=True)
    flat = mixed.reshape(wide_count, -1)
    spread = jnp.dot(
        wide_matrix,
        lax.all_to_all(flat, "wide", split_axis=0, concat_axis=0, tiled=True),
        precision=highest,
        preferred_element_type=jnp.float32,
    )
    owner_columns = half_width // wide_count
    spread = spread.reshape(wide_count, owner_columns, slab_total)
    slab_starts = (jnp.arange(wide_count, dtype=jnp.int32) * slab_total)[:, None]
    wanted = all_samples.reshape(wide_count, samples_slab) - slab_starts
    picked = jnp.take_along_axis(spread, wanted[:, None, :], axis=2)
    returned = lax.all_to_all(picked, "wide", split_axis=0, concat_axis=0, tiled=True)
    return (returned.reshape(half_width, samples_slab) * scale).T


def solution(mesh):
    return jax.shard_map(
        local,
        mesh=mesh,
        in_specs=(
            P("wide", "narrow", None, None),
            P("wide", None),
            P("wide"),
            P("wide", "narrow"),
            P("wide"),
        ),
        out_specs=P("wide", "narrow"),
        check_vma=False,
    )
```

profile of v0, /device:TPU:0, one launch (start us, length us, event | category | flops | bytes accessed | tf_op | source)
XLA Modules:
  0.0 328.6 jit_solution(9034065815628165564)
XLA Ops:
  6.5 0.0 reduce-scatter.2.cloned.1.call-start
  6.5 4.0 %fusion.99 = (f32[1024,512]{1,0:T(8,128)}, f32[1024,512]{1,0:T(8,128)S(1)}) fusion(f32[2048,512]{1,0:T(8,128)} %param.8), kind=kLoop, calls=%fused_computation.143 | loop fusion | bytes 8388608 | tf_op jit(solution)/shard_map/slice | solution.py:16
  10.5 3.0 collective-permute-start
  13.5 4.0 %collective-permute-start.1 = (f32[1024,512]{1,0:T(8,128)S(1)}, f32[1024,512]{1,0:T(8,128)}, u32[]{:S(2)}, u32[]{:S(2)}) collective-permute-start(f32[1024,512]{1,0:T(8,128)S(1)} %get-tuple-element.21), channel_id=1, source_target_pairs={{2,0},{4,2},{6,4},{8,6},{10,8},{12,10},{14,12},{16,14},{18,16},{20... | collective-permute-start | bytes 6291464 | tf_op jit(solution)/shard_map/ppermute | solution.py:19
  17.6 86.1 %collective-permute-done = f32[1024,512]{1,0:T(8,128)} collective-permute-done((f32[1024,512]{1,0:T(8,128)}, f32[1024,512]{1,0:T(8,128)}, u32[]{:S(2)}, u32[]{:S(2)}) %collective-permute-start) | collective-permute-done | bytes 2097184 | tf_op jit(solution)/shard_map/ppermute | solution.py:18
  103.7 1.9 collective-permute-done.1
  105.6 5.8 %pad_maximum_fusion = f32[4096,512]{1,0:T(8,128)} fusion(f32[1024,512]{1,0:T(8,128)} %collective-permute-done.1, f32[2048,512]{1,0:T(8,128)} %param.8, f32[1024,512]{1,0:T(8,128)} %collective-permute-done), kind=kLoop, calls=%fused_computation.8 | loop fusion | flops 4194304 | bytes 16777216 | tf_op jit(solution)/shard_map/concatenate | solution.py:20
  111.5 6.3 %gather_fusion.2 = f32[16,128,512]{2,1,0:T(8,128)} fusion(f32[32,128,512]{2,1,0:T(8,128)} %bitcast.85, s32[1024]{0:T(1024)S(1)} %get-tuple-element.39), kind=kCustom, calls=%fused_computation.1.clone | custom fusion | bytes 8388672 | tf_op jit(solution)/shard_map/jit(_take)/gather | solution.py:48
  117.7 6.2 %gather_fusion.5 = f32[16,128,512]{2,1,0:T(8,128)} fusion(f32[32,128,512]{2,1,0:T(8,128)} %bitcast.86, s32[1024]{0:T(1024)S(1)} %get-tuple-element.36), kind=kCustom, calls=%fused_computation.4.clone | custom fusion | bytes 8388672 | tf_op jit(solution)/shard_map/jit(_take)/gather | solution.py:48
  123.9 6.2 %gather_fusion.4 = f32[16,128,512]{2,1,0:T(8,128)} fusion(f32[32,128,512]{2,1,0:T(8,128)} %bitcast.87, s32[1024]{0:T(1024)S(1)} %get-tuple-element.37), kind=kCustom, calls=%fused_computation.3.clone | custom fusion | bytes 8388672 | tf_op jit(solution)/shard_map/jit(_take)/gather | solution.py:48
  130.0 6.1 %gather_fusion.3 = f32[16,128,512]{2,1,0:T(8,128)} fusion(f32[32,128,512]{2,1,0:T(8,128)} %bitcast.88, s32[1024]{0:T(1024)S(1)} %get-tuple-element.38), kind=kCustom, calls=%fused_computation.2.clone | custom fusion | bytes 8388672 | tf_op jit(solution)/shard_map/jit(_take)/gather | solution.py:48
  136.2 6.1 %gather_fusion.6 = f32[16,128,512]{2,1,0:T(8,128)} fusion(f32[32,128,512]{2,1,0:T(8,128)} %bitcast.89, s32[1024]{0:T(1024)S(1)} %get-tuple-element.35), kind=kCustom, calls=%fused_computation.5.clone | custom fusion | bytes 8388672 | tf_op jit(solution)/shard_map/jit(_take)/gather | solution.py:48
  142.3 6.2 %gather_fusion.7 = f32[16,128,512]{2,1,0:T(8,128)} fusion(f32[32,128,512]{2,1,0:T(8,128)} %bitcast.90, s32[1024]{0:T(1024)S(1)} %get-tuple-element.34), kind=kCustom, calls=%fused_computation.6.clone | custom fusion | bytes 8388672 | tf_op jit(solution)/shard_map/jit(_take)/gather | solution.py:48
  148.4 6.1 %gather_fusion.1 = f32[16,128,512]{2,1,0:T(8,128)} fusion(f32[32,128,512]{2,1,0:T(8,128)} %bitcast.91, s32[1024]{0:T(1024)S(1)} %pad_clamp_fusion.6), kind=kCustom, calls=%fused_computation.clone | custom fusion | bytes 8388672 | tf_op jit(solution)/shard_map/jit(_take)/gather | solution.py:48
  154.6 6.6 %fusion.10 = f32[16,512,128]{1,2,0:T(8,128)S(1)} fusion(f32[16,128,512]{2,1,0:T(8,128)} %gather_fusion.2, pred[16]{0:T(512)(128)(4,1)S(1)} %get-tuple-element.30, f32[16,7,128,128]{3,2,1,0:T(8,128)} %param.7), kind=kOutput, calls=%fused_computation.19 | convolution fusion | flops 1611661312 | bytes 9437200 | tf_op jit(solution)/shard_map/bik,bkn->nbi/dot_general | solution.py:49
  161.2 5.6 %fusion.4 = f32[16,512,128]{1,2,0:T(8,128)S(1)} fusion(f32[16,128,512]{2,1,0:T(8,128)S(1)} %copy-done.1, pred[16]{0:T(512)(128)(4,1)S(1)} %get-tuple-element.24, f32[16,7,128,128]{3,2,1,0:T(8,128)} %param.7), kind=kOutput, calls=%fused_computation.13 | convolution fusion | flops 1611661312 | bytes 9437200 | tf_op jit(solution)/shard_map/bik,bkn->nbi/dot_general | solution.py:49
  166.9 5.6 %fusion.6 = f32[16,512,128]{1,2,0:T(8,128)S(1)} fusion(f32[16,128,512]{2,1,0:T(8,128)S(1)} %copy-done.2, pred[16]{0:T(512)(128)(4,1)S(1)} %get-tuple-element.26, f32[16,7,128,128]{3,2,1,0:T(8,128)} %param.7), kind=kOutput, calls=%fused_computation.15 | convolution fusion | flops 1611661312 | bytes 9437200 | tf_op jit(solution)/shard_map/bik,bkn->nbi/dot_general | solution.py:49
  172.5 7.2 %fusion.8 = f32[16,512,128]{1,2,0:T(8,128)} fusion(f32[16,128,512]{2,1,0:T(8,128)S(1)} %copy-done.3, pred[16]{0:T(512)(128)(4,1)S(1)} %get-tuple-element.28, f32[16,7,128,128]{3,2,1,0:T(8,128)} %param.7), kind=kOutput, calls=%fused_computation.17 | convolution fusion | flops 1611661312 | bytes 9437200 | tf_op jit(solution)/shard_map/bik,bkn->nbi/dot_general | solution.py:49
  179.7 7.2 %fusion.2 = f32[16,512,128]{1,2,0:T(8,128)} fusion(f32[16,128,512]{2,1,0:T(8,128)S(1)} %copy-done, pred[16]{0:T(512)(128)(4,1)S(1)} %get-tuple-element.22, f32[16,7,128,128]{3,2,1,0:T(8,128)} %param.7), kind=kOutput, calls=%fused_computation.11 | convolution fusion | flops 1611661312 | bytes 9437200 | tf_op jit(solution)/shard_map/bik,bkn->nbi/dot_general | solution.py:49
  186.9 7.0 %fusion.12 = f32[16,512,128]{1,2,0:T(8,128)} fusion(f32[16,128,512]{2,1,0:T(8,128)S(1)} %copy-done.4, pred[16]{0:T(512)(128)(4,1)S(1)} %get-tuple-element.32, f32[16,7,128,128]{3,2,1,0:T(8,128)} %param.7), kind=kOutput, calls=%fused_computation.21 | convolution fusion | flops 1611661312 | bytes 9437200 | tf_op jit(solution)/shard_map/bik,bkn->nbi/dot_general | solution.py:49
  193.9 13.1 %add_add_fusion = f32[16,512,128]{1,2,0:T(8,128)} fusion(f32[16,512,128]{1,2,0:T(8,128)} %fusion.2, f32[16,512,128]{1,2,0:T(8,128)S(1)} %fusion.4, f32[16,512,128]{1,2,0:T(8,128)S(1)} %fusion.6, f32[16,512,128]{1,2,0:T(8,128)} %fusion.8, f32[16,512,128]{1,2,0:T(8,128)} %fusion.12, f32[16,512,128]{1,2,0:T(8,128)S(1)} %fusion.10, ...), kind=kOutput, calls=%fused_computation.23 | convolution fusion | flops 1617952768 | bytes 34603024 | tf_op jit(solution)/shard_map/bik,bkn->nbi/dot_general | solution.py:49
  207.1 0.0 reduce-scatter.2.cloned.1.call-update
  207.1 0.7 copy-done.5
  207.8 11.6 %reduce-scatter.2.cloned.1.call-done = f32[256,2048]{0,1:T(8,128)} async-done(((f32[512,2048]{0,1:T(8,128)}), f32[256,2048]{0,1:T(8,128)}) %reduce-scatter.2.cloned.1.call-update) | async-done | bytes 2097168 | tf_op jit(solution)/shard_map/reduce_scatter | solution.py:52
  219.4 1.9 broadcast_multiply_fusion
  221.3 2.0 copy.42
  223.3 4.8 %fusion.52 = f32[256,16,128]{2,1,0:T(8,128)} fusion(f32[256,16,128]{2,1,0:T(8,128)} %copy.42), kind=kOutput, calls=%fused_computation.65 | convolution fusion | flops 805879808 | bytes 4194304 | tf_op jit(solution)/shard_map/nbk,ik->nbi/dot_general | solution.py:60
  228.1 6.9 %all-to-all-start = ((f32[16,1,32768]{2,1,0:T(1,128)}), f32[16,1,32768]{2,1,0:T(1,128)S(1)}, u32[]{:S(2)}, u32[]{:S(2)}) async-start(f32[16,1,32768]{2,1,0:T(1,128)} %bitcast.93), calls=%async_computation.1 | async-start | bytes 4194304 | tf_op jit(solution)/shard_map/all_to_all | solution.py:72
  235.1 0.6 dynamic-slice
  236.3 0.2 dynamic-update-slice
  236.6 47.2 %all-reduce = s32[1024]{0:T(1024)S(1)} all-reduce(s32[1024]{0:T(1024)S(1)} %dynamic-update-slice), channel_id=1, replica_groups=mesh['wide'=16,'narrow'=2] {'wide'}, use_global_device_ids=true, to_apply=%add | all-reduce | flops 1024 | bytes 8192
  283.7 0.1 reshape.104
  283.8 0.1 reshape.100
  283.9 0.1 fusion.72
  284.0 0.1 reshape.161
  284.0 0.1 compare_and_fusion
  284.1 0.0 all-to-all-done
  284.1 1.2 copy.45
  285.3 1.9 fusion.16
  287.3 8.6 %copy.39 = f32[16,16,2048]{1,2,0:T(8,128)} copy(f32[16,16,2048]{2,0,1:T(8,128)S(1)} %fusion.16) | data formatting | bytes 4194304 | tf_op jit(solution)/shard_map/dot_general | solution.py:70
  295.8 10.5 %gather_fusion = f32[1024,16]{1,0:T(8,128)S(1)} fusion(f32[16,16,2048]{1,2,0:T(8,128)} %copy.39, s32[1024]{0:T(1024)S(1)} %reshape.161), kind=kCustom, calls=%fused_computation.7 | custom fusion | bytes 139264 | tf_op jit(solution)/shard_map/jit(take_along_axis)/gather | solution.py:80
  306.4 0.2 copy.40
  306.6 0.1 reshape.195
  306.7 12.9 %all_to_all.17 = f32[16,1,1024]{2,1,0:T(1,128)S(1)} all-to-all(f32[16,1,1024]{2,1,0:T(1,128)S(1)} %reshape.195), channel_id=1, replica_groups=mesh['wide'=16,'narrow'=2] {'wide'}, dimensions={0} | all-to-all | bytes 131072 | tf_op jit(solution)/shard_map/all_to_all | solution.py:81
  319.6 0.5 broadcast.268
  320.1 0.8 reduce
  320.9 0.1 reshape.196
  321.0 0.7 copy.41
  (28 shorter events, 0.1 us)
Async XLA Ops:
  6.5 11.0 %copy-start.6 = (s32[16,7]{0,1:T(8,128)S(1)}, s32[16,7]{0,1:T(8,128)}, u32[]{:S(2)}) copy-start(s32[16,7]{0,1:T(8,128)} %param.10) | copy-start | bytes 1348
  6.5 212.9 %reduce-scatter.2.cloned.1.call-start = ((), (), s32[]{:S(2)}) async-start(), calls=%async_computation.3 | async-start | bytes 6291456 | tf_op jit(solution)/shard_map/reduce_scatter | solution.py:52
  10.5 93.1 %collective-permute-start = (f32[1024,512]{1,0:T(8,128)}, f32[1024,512]{1,0:T(8,128)}, u32[]{:S(2)}, u32[]{:S(2)}) collective-permute-start(f32[1024,512]{1,0:T(8,128)} %get-tuple-element.20), channel_id=1, source_target_pairs={{0,2},{2,4},{4,6},{6,8},{8,10},{10,12},{12,14},{14,16},{16,18},{18... | collective-permute-start | bytes 6291464 | tf_op jit(solution)/shard_map/ppermute | solution.py:18
  13.5 92.1 %collective-permute-start.1 = (f32[1024,512]{1,0:T(8,128)S(1)}, f32[1024,512]{1,0:T(8,128)}, u32[]{:S(2)}, u32[]{:S(2)}) collective-permute-start(f32[1024,512]{1,0:T(8,128)S(1)} %get-tuple-element.21), channel_id=1, source_target_pairs={{2,0},{4,2},{6,4},{8,6},{10,8},{12,10},{14,12},{16,14},{18,16},{20... | collective-permute-start | bytes 6291464 | tf_op jit(solution)/shard_map/ppermute | solution.py:19
  154.6 6.6 %copy-start.1 = (f32[16,128,512]{2,1,0:T(8,128)S(1)}, f32[16,128,512]{2,1,0:T(8,128)}, u32[]{:S(2)}) copy-start(f32[16,128,512]{2,1,0:T(8,128)} %gather_fusion.5) | copy-start | bytes 12582916
  161.2 5.7 %copy-start.2 = (f32[16,128,512]{2,1,0:T(8,128)S(1)}, f32[16,128,512]{2,1,0:T(8,128)}, u32[]{:S(2)}) copy-start(f32[16,128,512]{2,1,0:T(8,128)} %gather_fusion.4) | copy-start | bytes 12582916
  166.9 5.7 %copy-start.3 = (f32[16,128,512]{2,1,0:T(8,128)S(1)}, f32[16,128,512]{2,1,0:T(8,128)}, u32[]{:S(2)}) copy-start(f32[16,128,512]{2,1,0:T(8,128)} %gather_fusion.3) | copy-start | bytes 12582916
  172.5 7.2 %copy-start = (f32[16,128,512]{2,1,0:T(8,128)S(1)}, f32[16,128,512]{2,1,0:T(8,128)}, u32[]{:S(2)}) copy-start(f32[16,128,512]{2,1,0:T(8,128)} %gather_fusion.6) | copy-start | bytes 12582916
  179.7 7.2 %copy-start.4 = (f32[16,128,512]{2,1,0:T(8,128)S(1)}, f32[16,128,512]{2,1,0:T(8,128)}, u32[]{:S(2)}) copy-start(f32[16,128,512]{2,1,0:T(8,128)} %gather_fusion.1) | copy-start | bytes 12582916
  207.1 0.7 copy-start.5
  223.3 11.7 %copy-start.8 = (u32[32]{0:T(128)S(1)}, u32[32]{0:T(128)}, u32[]{:S(2)}) copy-start(u32[32]{0:T(128)} %constant.111) | copy-start | bytes 388
  223.3 13.0 %copy-start.7 = (s32[64]{0:T(128)S(1)}, s32[64]{0:T(128)}, u32[]{:S(2)}) copy-start(s32[64]{0:T(128)} %param.11) | copy-start | bytes 772
  228.1 56.0 %all-to-all-start = ((f32[16,1,32768]{2,1,0:T(1,128)}), f32[16,1,32768]{2,1,0:T(1,128)S(1)}, u32[]{:S(2)}, u32[]{:S(2)}) async-start(f32[16,1,32768]{2,1,0:T(1,128)} %bitcast.93), calls=%async_computation.1 | async-start | bytes 4194304 | tf_op jit(solution)/shard_map/all_to_all | solution.py:72
Sparse Core Ops, SparseCore 0:
  207.2 12.1 reduce-scatter.1
where the time goes:
time: 329 us
  waiting for transfers between devices  99.7 us (30%)
  local copies, waits for them, and re-layouts  72.8 us (22%)
  blocking collectives  60 us (18%)
  matrix products  59.1 us (18%)
  between operations  14.3 us (4%)
  starting transfers between devices  13.9 us (4%)
  other arithmetic  8.82 us (3%)
    ppermute x1, waiting for transfers between devices, extended_2(): before = lax.ppermute(last, axis, up)  86.1 us
    dot_general x7, matrix products, local(): jnp.einsum('bik,bkn->nbi', blocks[:, slot_number], picked, precision=high...  52.4 us
    unnamed x1, blocking collectives  47.2 us
    gather x7, local copies, waits for them, and re-layouts, local(): picked = jnp.take(ext_blocks, local_columns[:, slot_number], axis=0)  43.1 us
    all_to_all x1, blocking collectives, local(): lax.all_to_all(picked, 'wide', split_axis=0, concat_axis=0, tiled=True)  12.9 us
    reduce_scatter x1, waiting for transfers between devices, local(): lax.psum_scatter(running.reshape(half_width * lax.axis_size('narrow'), sl...  11.6 us
    gather x3, local copies, waits for them, and re-layouts, local(): picked = jnp.take_along_axis(spread, wanted[:, None, :], axis=2)  10.8 us
    dot_general x1, local copies, waits for them, and re-layouts, local(): jnp.dot(wide_matrix, lax.all_to_all(flat, 'wide', split_axis=0, concat_ax...  8.57 us
  transfers between devices with their start and end apart: 4, of which 3 were waited for; matrix products, arithmetic and copies ran while one was open for 0% of the time, Pallas kernels for 0%

commit v1 on v0

v1 whole, which is shorter than its diff:
```python
import functools
import math

import jax
import jax.numpy as jnp
from jax import lax
from jax.experimental import pallas as pl
from jax.experimental.pallas import tpu as pltpu
from jax.sharding import PartitionSpec as P

REACH = 8
MESH = pl.DeviceIdType.MESH


def split_bf16(x):
    high = x.astype(jnp.bfloat16)
    return high, (x - high.astype(jnp.float32)).astype(jnp.bfloat16)


def sketch_kernel(shares, slots, order, *refs):
    columns = refs[:shares]
    blocks = refs[shares:2 * shares]
    before, inside, after, signs, rows_mix, rows_block, out = refs[2 * shares:2 * shares + 7]
    high, low = refs[2 * shares + 7:]
    b = pl.program_id(0)
    half = high.shape[2]

    @pl.when(b == 0)
    def _():
        out[...] = jnp.zeros_like(out)
        start = 0
        for piece in (before, inside, after):
            def convert(i, carry, piece=piece, start=start):
                h, l = split_bf16(piece[pl.ds(pl.multiple_of(i * order, order), order), :])
                high[start + i] = h
                low[start + i] = l
                return carry
            count = piece.shape[0] // order
            lax.fori_loop(0, count, convert, 0)
            start += count

    total = jnp.zeros((order, half), jnp.float32)
    pairs = [(share, j) for j in range(slots) for share in range(shares)]
    for at in range(0, len(pairs), 2):
        group = pairs[at:at + 2]
        a = jnp.concatenate([blocks[share][0, j] for share, j in group], axis=1)
        a_high, a_low = split_bf16(a)
        where = [columns[share][b, j] for share, j in group]
        v_high = jnp.concatenate([high[w] for w in where], axis=0)
        v_low = jnp.concatenate([low[w] for w in where], axis=0)
        both = jnp.dot(
            jnp.concatenate([a_high, a_low], axis=0), v_high, preferred_element_type=jnp.float32
        )
        small = jnp.dot(a_high, v_low, preferred_element_type=jnp.float32)
        total = total + (both[:order] + (both[order:] + small))
    p_high, p_low = split_bf16(total)
    stacked = jnp.concatenate([p_high, p_low], axis=0)
    sign = (2 * signs[0] - 1).astype(jnp.float32)
    step = min(256, out.shape[0])

    def mix(i, carry):
        rows = pl.ds(pl.multiple_of(i * step, step), step)
        r = jnp.where(rows_block[rows, :] == b, rows_mix[rows, :] * sign, 0.0).astype(jnp.bfloat16)
        out[rows, :] += jnp.dot(
            jnp.concatenate([r, r], axis=1), stacked, preferred_element_type=jnp.float32
        )
        return carry
    lax.fori_loop(0, out.shape[0] // step, mix, 0, unroll=out.shape[0] // step <= 4)


def scatter_kernel(count, scale, x, out, held, send_sem, recv_sem):
    me = lax.axis_index("wide")

    def copy(p):
        to = (me + p) % count
        return pltpu.make_async_remote_copy(
            src_ref=x.at[to],
            dst_ref=held.at[p],
            send_sem=send_sem.at[p],
            recv_sem=recv_sem.at[p],
            device_id={"wide": to},
            device_id_type=MESH,
        )

    def begin(p, carry):
        copy(p).start()
        return carry

    def end(p, carry):
        copy(p).wait()
        out[...] += held[p]
        return carry
    lax.fori_loop(1, count, begin, 0)
    out[...] = x[me]
    lax.fori_loop(1, count, end, 0)
    out[...] = out[...] * scale


def parity_sign(bits):
    return (1 - 2 * (lax.population_count(bits) & 1)).astype(jnp.float32)


def local(blocks, vectors, sign_bits, column_blocks, sample_rows):
    slab_rows, slots, order = blocks.shape[:3]
    width = vectors.shape[1]
    wide_count = lax.axis_size("wide")
    shares = lax.axis_size("narrow")
    half = width // shares
    me = lax.axis_index("wide")
    total_blocks = slab_rows * wide_count
    slab_total = slab_rows * order
    samples_slab = sample_rows.shape[0]
    samples = samples_slab * wide_count

    inside = lax.dynamic_slice_in_dim(vectors, lax.axis_index("narrow") * half, half, axis=1)
    reach_rows = REACH * order
    up = [(i, (i + 1) % wide_count) for i in range(wide_count)]
    down = [(j, i) for i, j in up]
    before = lax.ppermute(inside[slab_total - reach_rows:], "wide", up)
    after = lax.ppermute(inside[:reach_rows], "wide", down)

    local_columns = (column_blocks - me * slab_rows + REACH) % total_blocks
    all_blocks, all_columns = [blocks], [local_columns]
    for shift in range(1, shares):
        pairs = [(i, (i + shift) % shares) for i in range(shares)]
        all_blocks.append(lax.ppermute(blocks, "narrow", pairs))
        all_columns.append(lax.ppermute(local_columns, "narrow", pairs))

    gathered = sample_rows[None]
    reach = 1
    while reach < wide_count:
        pairs = [(i, i ^ reach) for i in range(wide_count)]
        gathered = jnp.concatenate([gathered, lax.ppermute(gathered, "wide", pairs)], axis=0)
        reach *= 2
    order_of = jnp.arange(wide_count, dtype=jnp.int32) ^ me
    picked = jnp.take(gathered, order_of, axis=0).reshape(samples, 1)
    slab_of = picked // slab_total
    inner = picked - slab_of * slab_total
    positions = jnp.arange(order, dtype=jnp.int32)[None]
    rows_mix = parity_sign(positions & inner) * parity_sign(slab_of & me)
    rows_block = jnp.broadcast_to(inner // order, (samples, order))

    def whole(shape):
        return pl.BlockSpec(shape, lambda b, *_: (0,) * len(shape), pipeline_mode=pl.Buffered(1))
    partial = pl.pallas_call(
        functools.partial(sketch_kernel, shares, slots, order),
        grid_spec=pltpu.PrefetchScalarGridSpec(
            num_scalar_prefetch=shares,
            grid=(slab_rows,),
            in_specs=[
                pl.BlockSpec((1, slots, order, order), lambda b, *_: (b, 0, 0, 0))
                for _ in range(shares)
            ] + [
                whole((reach_rows, half)),
                whole((slab_total, half)),
                whole((reach_rows, half)),
                pl.BlockSpec((1, 1, order), lambda b, *_: (b, 0, 0)),
                whole((samples, order)),
                whole((samples, order)),
            ],
            out_specs=pl.BlockSpec((samples, half), lambda b, *_: (0, 0)),
            scratch_shapes=[
                pltpu.VMEM((slab_rows + 2 * REACH, order, half), jnp.bfloat16),
                pltpu.VMEM((slab_rows + 2 * REACH, order, half), jnp.bfloat16),
            ],
        ),
        out_shape=jax.ShapeDtypeStruct((samples, half), jnp.float32),
        name="sketch",
    )(*all_columns, *all_blocks, before, inside, after,
      sign_bits.reshape(slab_rows, 1, order), rows_mix, rows_block)

    scale = math.sqrt(slab_total * wide_count / samples) / math.sqrt(order * wide_count)
    return pl.pallas_call(
        functools.partial(scatter_kernel, wide_count, scale),
        in_specs=[pl.BlockSpec(memory_space=pltpu.VMEM)],
        out_specs=pl.BlockSpec(memory_space=pltpu.VMEM),
        out_shape=jax.ShapeDtypeStruct((samples_slab, half), jnp.float32),
        scratch_shapes=[
            pltpu.VMEM((wide_count, samples_slab, half), jnp.float32),
            pltpu.SemaphoreType.DMA((wide_count,)),
            pltpu.SemaphoreType.DMA((wide_count,)),
        ],
        compiler_params=pltpu.CompilerParams(has_side_effects=True),
        name="scatter",
    )(partial.reshape(wide_count, samples_slab, half))


def solution(mesh):
    return jax.shard_map(
        local,
        mesh=mesh,
        in_specs=(
            P("wide", "narrow", None, None),
            P("wide", None),
            P("wide"),
            P("wide", "narrow"),
            P("wide"),
        ),
        out_specs=P("wide", "narrow"),
        check_vma=False,
    )
```

time: 329 us -> 114 us (0.35)
  the two profiles are of different devices: /device:TPU:0 before, /device:TPU:14 now
where the time goes in v1:
time: 114 us
  Pallas kernels  58.8 us (52%)
  waiting for transfers between devices  36.4 us (32%)
  starting transfers between devices  8.79 us (8%)
  local copies, waits for them, and re-layouts  8.51 us (7%)
  other arithmetic  1.33 us (1%)
    pallas_call x1, Pallas kernels, local(): pl.pallas_call(functools.partial(scatter_kernel, wide_count, scale), in_s...  35.1 us
    pallas_call x1, Pallas kernels, local(): pl.pallas_call(functools.partial(sketch_kernel, shares, slots, order), gr...  23.7 us
    ppermute x4, waiting for transfers between devices, local(): lax.ppermute(gathered, 'wide', pairs)  22.9 us
    ppermute x1, waiting for transfers between devices, local(): after = lax.ppermute(inside[:reach_rows], 'wide', down)  12.7 us
    ppermute x4, starting transfers between devices, local(): lax.ppermute(gathered, 'wide', pairs)  4.67 us
    slice x1, local copies, waits for them, and re-layouts, local(): after = lax.ppermute(inside[:reach_rows], 'wide', down)  2.8 us
    ppermute x1, starting transfers between devices, local(): before = lax.ppermute(inside[slab_total - reach_rows:], 'wide', up)  2.33 us
  transfers between devices with their start and end apart: 8, of which 5 were waited for; matrix products, arithmetic and copies ran while one was open for 6% of the time, Pallas kernels for 0%

profile of v1, /device:TPU:14, one launch (start us, length us, event | category | flops | bytes accessed | tf_op | source)
XLA Modules:
  0.0 113.8 jit_solution(13975197893163589045)
XLA Ops:
  0.0 0.0 collective-permute-start.1
  0.0 0.5 collective-permute-start.4
  0.5 0.8 copy.6
  1.3 0.0 copy-start.3
  1.3 0.3 collective-permute-start
  1.6 0.0 copy-start
  1.6 0.0 copy-start.5
  1.6 2.8 %constant_dynamic-slice_fusion = (f32[1024,256]{1,0:T(8,128)}, f32[1024,256]{1,0:T(8,128)S(1)}) fusion(f32[2048,512]{1,0:T(8,128)} %param.6, s32[]{:T(128)S(6)} %select_n.96, s32[]{:T(128)S(6)} %add.60), kind=kLoop, calls=%fused_computation.31 | loop fusion | bytes 4194312 | tf_op jit(solution)/shard_map/slice | solution.py:120
  4.4 1.5 %collective-permute-start.3 = (f32[1024,256]{1,0:T(8,128)}, f32[1024,256]{1,0:T(8,128)S(1)}, u32[]{:S(2)}, u32[]{:S(2)}) collective-permute-start(f32[1024,256]{1,0:T(8,128)} %get-tuple-element.7), channel_id=1, source_target_pairs={{2,0},{4,2},{6,4},{8,6},{10,8},{12,10},{14,12},{16,14},{18,16},{20... | collective-permute-start | bytes 3145736 | tf_op jit(solution)/shard_map/ppermute | solution.py:120
  5.9 2.3 %collective-permute-start.2 = (f32[1024,256]{1,0:T(8,128)S(1)}, f32[1024,256]{1,0:T(8,128)S(1)}, u32[]{:S(2)}, u32[]{:S(2)}) collective-permute-start(f32[1024,256]{1,0:T(8,128)S(1)} %get-tuple-element.8), channel_id=1, source_target_pairs={{0,2},{2,4},{4,6},{6,8},{8,10},{10,12},{12,14},{14,16},{16,18},{18... | collective-permute-start | bytes 3145736 | tf_op jit(solution)/shard_map/ppermute | solution.py:119
  8.2 0.0 copy-done
  8.2 1.6 %constant_dynamic-slice_fusion.1.refs_5_ = f32[2048,256]{1,0:T(8,128)} fusion(f32[2048,512]{1,0:T(8,128)S(1)} %copy-done, s32[]{:T(128)S(6)} %select_n.96), kind=kLoop, calls=%fused_computation.32 | loop fusion | bytes 4194308 | tf_op jit(solution)/shard_map/dynamic_slice | solution.py:115
  9.9 0.0 copy-done.3
  9.9 0.0 collective-permute-done.4
  9.9 0.0 copy-done.5
  9.9 0.1 collective-permute-start.5
  10.0 3.6 %collective-permute-done.5 = s32[2,64]{1,0:T(2,128)S(1)} collective-permute-done((s32[2,64]{1,0:T(2,128)S(1)}, s32[2,64]{1,0:T(2,128)S(1)}, u32[]{:S(2)}, u32[]{:S(2)}) %collective-permute-start.5) | collective-permute-done | bytes 544 | tf_op jit(solution)/shard_map/ppermute | solution.py:133
  13.6 0.5 collective-permute-start.6
  14.1 17.7 %collective-permute-done.6 = s32[4,64]{1,0:T(4,128)S(1)} collective-permute-done((s32[4,64]{1,0:T(4,128)S(1)}, s32[4,64]{1,0:T(4,128)S(1)}, u32[]{:S(2)}, u32[]{:S(2)}) %collective-permute-start.6) | collective-permute-done | bytes 1056 | tf_op jit(solution)/shard_map/ppermute | solution.py:133
  31.8 3.5 %collective-permute-start.7 = (s32[8,64]{1,0:T(8,128)S(1)}, s32[8,64]{1,0:T(8,128)S(1)}, u32[]{:S(2)}, u32[]{:S(2)}) collective-permute-start(s32[8,64]{1,0:T(8,128)S(1)} %pad_add_fusion), channel_id=1, source_target_pairs={{0,16},{2,18},{4,20},{6,22},{8,24},{10,26},{12,28},{14,30},{16,0},... | collective-permute-start | bytes 6152 | tf_op jit(solution)/shard_map/ppermute | solution.py:133
  35.4 1.6 %collective-permute-done.7 = s32[8,64]{1,0:T(8,128)S(1)} collective-permute-done((s32[8,64]{1,0:T(8,128)S(1)}, s32[8,64]{1,0:T(8,128)S(1)}, u32[]{:S(2)}, u32[]{:S(2)}) %collective-permute-start.7) | collective-permute-done | bytes 2080 | tf_op jit(solution)/shard_map/ppermute | solution.py:133
  37.0 0.6 gather_fusion
  37.6 0.1 broadcast_select_fusion
  37.6 0.1 select_n.100
  37.7 1.2 %convert_multiply_fusion.refs_8_ = f32[1024,128]{1,0:T(8,128)} fusion(f32[1024]{0:T(1024)S(1)} %get-tuple-element.9, s32[1024]{0:T(1024)S(1)} %get-tuple-element.6), kind=kLoop, calls=%fused_computation.1 | loop fusion | flops 917504 | bytes 532480 | tf_op jit(solution)/shard_map/mul | solution.py:140
  38.9 0.0 collective-permute-done.refs_1_
  38.9 0.0 copy-start.4
  38.9 12.7 %collective-permute-done.3.refs_6_ = f32[1024,256]{1,0:T(8,128)S(1)} collective-permute-done((f32[1024,256]{1,0:T(8,128)}, f32[1024,256]{1,0:T(8,128)S(1)}, u32[]{:S(2)}, u32[]{:S(2)}) %collective-permute-start.3) | collective-permute-done | bytes 1048608 | tf_op jit(solution)/shard_map/ppermute | solution.py:120
  51.6 0.0 copy-start.1
  51.6 0.8 collective-permute-done.2.refs_4_
  52.4 0.0 copy-start.2
  52.4 0.0 collective-permute-done.1.refs_3_
  52.4 1.2 %broadcast_in_dim.22.refs_9_ = s32[1024,128]{1,0:T(8,128)} broadcast(s32[1024]{0:T(1024)S(1)} %get-tuple-element.5), dimensions={0} | broadcast | bytes 528384 | tf_op jit(solution)/shard_map/broadcast_in_dim | solution.py:141
  53.6 0.0 copy-done.4
  53.6 0.0 copy-done.1
  53.6 0.0 copy-done.2
  53.6 23.7 %sketch.1 = f32[1024,256]{1,0:T(8,128)} custom-call(s32[16,7]{1,0:T(8,128)} %copy-done.3, s32[16,7]{1,0:T(8,128)} %copy-done.4, f32[16,7,128,128]{3,2,1,0:T(8,128)} %refs_2_.1, f32[16,7,128,128]{3,2,1,0:T(8,128)} %collective-permute-done.1.refs_3_, f32[1024,256]{1,0:T(8,128)} %copy-done.2, f32[2048,256]{1,0:T(8,128)} %constant_dynamic-slice_fusion.1.refs_5_, ...), custom_call_target="tpu_custom_call" | custom-call | tf_op jit(solution)/shard_map/sketch/pallas_call | solution.py:145
  77.3 35.1 %scatter.1 = f32[64,256]{1,0:T(8,128)} custom-call(f32[16,64,256]{2,1,0:T(8,128)} %bitcast.5), custom_call_target="tpu_custom_call" | custom-call | tf_op jit(solution)/shard_map/scatter/pallas_call | solution.py:173
  112.4 1.5 %copy.8 = f32[64,256]{1,0:T(8,128)} copy(f32[64,256]{1,0:T(8,128)} %scatter.1) | data formatting | bytes 131072
  (9 shorter events, 0.1 us)
Async XLA Ops:
  0.0 52.4 %collective-permute-start.1 = (f32[16,7,128,128]{3,2,1,0:T(8,128)}, f32[16,7,128,128]{3,2,1,0:T(8,128)}, u32[]{:S(2)}, u32[]{:S(2)}) collective-permute-start(f32[16,7,128,128]{3,2,1,0:T(8,128)} %refs_2_.1), channel_id=1, source_target_pairs={{0,1},{1,0},{2,3},{3,2},{4,5},{5,4},{6,7},{7,6},{8,9},{9,8},{10,11... | collective-permute-start | bytes 22020104 | tf_op jit(solution)/shard_map/ppermute | solution.py:126
  0.0 9.9 %collective-permute-start.4 = (s32[1,64]{1,0:T(1,128)}, s32[1,64]{1,0:T(1,128)S(1)}, u32[]{:S(2)}, u32[]{:S(2)}) collective-permute-start(s32[1,64]{1,0:T(1,128)} %bitcast.7), channel_id=1, source_target_pairs={{0,2},{2,0},{4,6},{6,4},{8,10},{10,8},{12,14},{14,12},{16,18},{18,... | collective-permute-start | bytes 776 | tf_op jit(solution)/shard_map/ppermute | solution.py:133
  1.3 8.6 %copy-start.3 = (s32[16,7]{1,0:T(8,128)}, s32[16,7]{1,0:T(8,128)S(1)}, u32[]{:S(2)}) copy-start(s32[16,7]{1,0:T(8,128)S(1)} %add_select_fusion.refs_0_) | copy-start | bytes 1348
  1.3 37.6 %collective-permute-start = (s32[16,7]{1,0:T(8,128)S(1)}, s32[16,7]{1,0:T(8,128)S(1)}, u32[]{:S(2)}, u32[]{:S(2)}) collective-permute-start(s32[16,7]{1,0:T(8,128)S(1)} %add_select_fusion.refs_0_), channel_id=1, source_target_pairs={{0,1},{1,0},{2,3},{3,2},{4,5},{5,4},{6,7},{7,6},{8,9},{9,8},{10,11... | collective-permute-start | bytes 1352 | tf_op jit(solution)/shard_map/ppermute | solution.py:127
  1.6 6.6 %copy-start = (f32[2048,512]{1,0:T(8,128)S(1)}, f32[2048,512]{1,0:T(8,128)}, u32[]{:S(2)}) copy-start(f32[2048,512]{1,0:T(8,128)} %param.6) | copy-start | bytes 12582916
  1.6 8.3 %copy-start.5 = (s32[64]{0:T(128)S(1)}, s32[64]{0:T(128)}, u32[]{:S(2)}) copy-start(s32[64]{0:T(128)} %param.9) | copy-start | bytes 772
  4.4 47.1 %collective-permute-start.3 = (f32[1024,256]{1,0:T(8,128)}, f32[1024,256]{1,0:T(8,128)S(1)}, u32[]{:S(2)}, u32[]{:S(2)}) collective-permute-start(f32[1024,256]{1,0:T(8,128)} %get-tuple-element.7), channel_id=1, source_target_pairs={{2,0},{4,2},{6,4},{8,6},{10,8},{12,10},{14,12},{16,14},{18,16},{20... | collective-permute-start | bytes 3145736 | tf_op jit(solution)/shard_map/ppermute | solution.py:120
  5.9 46.5 %collective-permute-start.2 = (f32[1024,256]{1,0:T(8,128)S(1)}, f32[1024,256]{1,0:T(8,128)S(1)}, u32[]{:S(2)}, u32[]{:S(2)}) collective-permute-start(f32[1024,256]{1,0:T(8,128)S(1)} %get-tuple-element.8), channel_id=1, source_target_pairs={{0,2},{2,4},{4,6},{6,8},{8,10},{10,12},{12,14},{14,16},{16,18},{18... | collective-permute-start | bytes 3145736 | tf_op jit(solution)/shard_map/ppermute | solution.py:119
  9.9 3.7 %collective-permute-start.5 = (s32[2,64]{1,0:T(2,128)S(1)}, s32[2,64]{1,0:T(2,128)S(1)}, u32[]{:S(2)}, u32[]{:S(2)}) collective-permute-start(s32[2,64]{1,0:T(2,128)S(1)} %pad_add_fusion.2), channel_id=1, source_target_pairs={{0,4},{2,6},{4,0},{6,2},{8,12},{10,14},{12,8},{14,10},{16,20},{18,... | collective-permute-start | bytes 1544 | tf_op jit(solution)/shard_map/ppermute | solution.py:133
  13.6 18.2 %collective-permute-start.6 = (s32[4,64]{1,0:T(4,128)S(1)}, s32[4,64]{1,0:T(4,128)S(1)}, u32[]{:S(2)}, u32[]{:S(2)}) collective-permute-start(s32[4,64]{1,0:T(4,128)S(1)} %pad_add_fusion.1), channel_id=1, source_target_pairs={{0,8},{2,10},{4,12},{6,14},{8,0},{10,2},{12,4},{14,6},{16,24},{18,... | collective-permute-start | bytes 3080 | tf_op jit(solution)/shard_map/ppermute | solution.py:133
  31.8 5.1 %collective-permute-start.7 = (s32[8,64]{1,0:T(8,128)S(1)}, s32[8,64]{1,0:T(8,128)S(1)}, u32[]{:S(2)}, u32[]{:S(2)}) collective-permute-start(s32[8,64]{1,0:T(8,128)S(1)} %pad_add_fusion), channel_id=1, source_target_pairs={{0,16},{2,18},{4,20},{6,22},{8,24},{10,26},{12,28},{14,30},{16,0},... | collective-permute-start | bytes 6152 | tf_op jit(solution)/shard_map/ppermute | solution.py:133
  38.9 14.7 %copy-start.4 = (s32[16,7]{1,0:T(8,128)}, s32[16,7]{1,0:T(8,128)S(1)}, u32[]{:S(2)}) copy-start(s32[16,7]{1,0:T(8,128)S(1)} %collective-permute-done.refs_1_) | copy-start | bytes 1348
  51.6 2.0 %copy-start.1 = (f32[1024,256]{1,0:T(8,128)}, f32[1024,256]{1,0:T(8,128)S(1)}, u32[]{:S(2)}) copy-start(f32[1024,256]{1,0:T(8,128)S(1)} %collective-permute-done.3.refs_6_) | copy-start | bytes 3145732
  52.4 1.2 %copy-start.2 = (f32[1024,256]{1,0:T(8,128)}, f32[1024,256]{1,0:T(8,128)S(1)}, u32[]{:S(2)}) copy-start(f32[1024,256]{1,0:T(8,128)S(1)} %collective-permute-done.2.refs_4_) | copy-start | bytes 3145732

commit v2 on v1

v2 whole, which is shorter than its diff:
```python
import functools
import math

import jax
import jax.numpy as jnp
from jax import lax
from jax.experimental import pallas as pl
from jax.experimental.pallas import tpu as pltpu
from jax.sharding import PartitionSpec as P

REACH = 8
MESH = pl.DeviceIdType.MESH


def split_bf16(x):
    high = x.astype(jnp.bfloat16)
    return high, (x - high.astype(jnp.float32)).astype(jnp.bfloat16)


def add_pairs(first, last, b, r, slots, order, which, columns, blocks, high, low, shift, total):
    def block(at):
        which_at = which[b, at]
        found = blocks[0][r, which_at % slots]
        for share in range(1, len(blocks)):
            found = jnp.where(which_at // slots == share, blocks[share][r, which_at % slots], found)
        return found

    def pair(i, carry):
        one = first + 2 * i
        two = jnp.minimum(one + 1, last - 1)
        kept = (one + 1 < last).astype(jnp.float32)
        a = jnp.concatenate([block(one), block(two) * kept], axis=1)
        a_high, a_low = split_bf16(a)
        where = [shift(columns[b, at]) for at in (one, two)]
        v_high = jnp.concatenate([high[w] for w in where], axis=0)
        v_low = jnp.concatenate([low[w] for w in where], axis=0)
        both = jnp.dot(
            jnp.concatenate([a_high, a_low], axis=0), v_high, preferred_element_type=jnp.float32
        )
        small = jnp.dot(a_high, v_low, preferred_element_type=jnp.float32)
        total[...] += both[:order] + (both[order:] + small)
        return carry
    lax.fori_loop(0, (last - first + 1) // 2, pair, 0)


def convert_rows(piece, start, order, high, low):
    def convert(i, carry):
        h, l = split_bf16(piece[pl.ds(pl.multiple_of(i * order, order), order), :])
        high[start + i] = h
        low[start + i] = l
        return carry
    lax.fori_loop(0, piece.shape[0] // order, convert, 0)


def inside_kernel(shares, slots, order, which, columns, near, place, *refs):
    blocks, (inside, out, high, low) = refs[:shares], refs[shares:]
    step_rows = blocks[0].shape[0]
    step = pl.program_id(0)

    @pl.when(step == 0)
    def _():
        convert_rows(inside, 0, order, high, low)
    out[...] = jnp.zeros_like(out)

    def row(r, carry):
        b = step * step_rows + r
        add_pairs(
            0, near[b], b, r, slots, order, which, columns, blocks, high, low,
            lambda c: c - REACH, out.at[pl.ds(pl.multiple_of(r * order, order), order), :]
        )
        return carry
    lax.fori_loop(0, step_rows, row, 0)


def sketch_kernel(shares, slots, order, which, columns, near, rows, row_signs, *refs):
    blocks = refs[:shares]
    before, after, product, signs, hadamard, out, high, low, total, mixed = refs[shares:]
    step_rows = blocks[0].shape[0]
    slab_rows = signs.shape[0]
    step = pl.program_id(0)

    @pl.when(step == 0)
    def _():
        convert_rows(before, 0, order, high, low)
        convert_rows(after, REACH, order, high, low)

    def row(r, carry):
        b = step * step_rows + r
        total[...] = product[pl.ds(pl.multiple_of(r * order, order), order), :]
        add_pairs(
            near[b], which.shape[1], b, r, slots, order, which, columns, blocks, high, low,
            lambda c: jnp.where(c < REACH, c, c - slab_rows), total
        )
        stacked = jnp.concatenate(split_bf16(total[...]), axis=0)
        mix = (hadamard[...] * (2 * signs[b] - 1).astype(jnp.float32)).astype(jnp.bfloat16)
        mixed[pl.ds(pl.multiple_of(b * order, order), order), :] = jnp.dot(
            jnp.concatenate([mix, mix], axis=1), stacked, preferred_element_type=jnp.float32
        )
        return carry
    lax.fori_loop(0, step_rows, row, 0)

    @pl.when(step == pl.num_programs(0) - 1)
    def _():
        per_slab = out.shape[0] // row_signs.shape[0]
        group = 8

        def pick(i, carry):
            first = i * group
            sign = row_signs[first // per_slab]
            picked = [mixed[pl.ds(rows[first + k], 1), :] for k in range(group)]
            out[pl.ds(pl.multiple_of(first, group), group), :] = jnp.concatenate(picked, axis=0) * sign
            return carry
        lax.fori_loop(0, out.shape[0] // group, pick, 0, unroll=4)


def scatter_kernel(scale, x, out, held, total, last, send_sem, recv_sem, send_last, recv_last):
    far_count, near_count = x.shape[:2]
    me = lax.axis_index("wide")
    far_me, near_me = me // near_count, me % near_count

    def near_copy(p):
        to = (near_me + p) % near_count
        return pltpu.make_async_remote_copy(
            src_ref=x.at[:, to],
            dst_ref=held.at[p],
            send_sem=send_sem.at[p],
            recv_sem=recv_sem.at[p],
            device_id={"wide": far_me * near_count + to},
            device_id_type=MESH,
        )

    def far_copy(p):
        to = (far_me + p) % far_count
        return pltpu.make_async_remote_copy(
            src_ref=total.at[to],
            dst_ref=last.at[p],
            send_sem=send_last.at[p],
            recv_sem=recv_last.at[p],
            device_id={"wide": to * near_count + near_me},
            device_id_type=MESH,
        )

    def begin(copy):
        def body(p, carry):
            copy(p).start()
            return carry
        return body

    def end_near(p, carry):
        near_copy(p).wait()
        total[...] += held[p]
        return carry

    def end_far(p, carry):
        far_copy(p).wait()
        out[...] += last[p]
        return carry
    lax.fori_loop(1, near_count, begin(near_copy), 0)
    total[...] = x[:, near_me]
    lax.fori_loop(1, near_count, end_near, 0)
    lax.fori_loop(1, far_count, begin(far_copy), 0)
    out[...] = total[far_me]
    lax.fori_loop(1, far_count, end_far, 0)
    out[...] = out[...] * scale


def parity_sign(bits):
    return (1 - 2 * (lax.population_count(bits) & 1)).astype(jnp.float32)


def local(blocks, vectors, sign_bits, column_blocks, sample_rows):
    slab_rows, slots, order = blocks.shape[:3]
    width = vectors.shape[1]
    wide_count = lax.axis_size("wide")
    shares = lax.axis_size("narrow")
    half = width // shares
    me = lax.axis_index("wide")
    total_blocks = slab_rows * wide_count
    slab_total = slab_rows * order
    samples_slab = sample_rows.shape[0]
    samples = samples_slab * wide_count

    def widen(gathered, reach):
        radix = min(4, wide_count // reach)
        parts = [gathered]
        for k in range(1, radix):
            pairs = [(i, i ^ (k * reach)) for i in range(wide_count)]
            parts.append(lax.ppermute(gathered, "wide", pairs))
        return jnp.concatenate(parts, axis=0), reach * radix
    gathered, reach = widen(sample_rows[None], 1)
    narrow_me = lax.axis_index("narrow")
    reach_rows = REACH * order
    up = [(i, (i + 1) % wide_count) for i in range(wide_count)]
    down = [(j, i) for i, j in up]
    last_rows = lax.dynamic_slice(
        vectors, (slab_total - reach_rows, narrow_me * half), (reach_rows, half)
    )
    first_rows = lax.dynamic_slice(vectors, (0, narrow_me * half), (reach_rows, half))
    before = lax.ppermute(last_rows, "wide", up)
    after = lax.ppermute(first_rows, "wide", down)

    local_columns = (column_blocks - me * slab_rows + REACH) % total_blocks
    all_blocks, all_columns = [blocks], [local_columns]
    for shift in range(1, shares):
        pairs = [(i, (i + shift) % shares) for i in range(shares)]
        all_blocks.append(lax.ppermute(blocks, "narrow", pairs))
        all_columns.append(lax.ppermute(local_columns, "narrow", pairs))
    columns = jnp.concatenate(all_columns, axis=1)

    entries = shares * slots
    inside = ((columns >= REACH) & (columns < REACH + slab_rows)).astype(jnp.int32)
    places = jnp.arange(entries, dtype=jnp.int32)
    ahead = (places[None, :] < places[:, None]).astype(jnp.int32)[None]
    near = jnp.sum(inside, axis=1)
    rank = jnp.where(
        inside == 1,
        jnp.sum(inside[:, None, :] * ahead, axis=2),
        near[:, None] + jnp.sum((1 - inside)[:, None, :] * ahead, axis=2),
    )
    chosen = (rank[:, None, :] == places[None, :, None]).astype(jnp.int32)
    which = jnp.sum(chosen * places[None, None, :], axis=2)
    columns = jnp.sum(chosen * columns[:, None, :], axis=2)

    positions = jnp.arange(order, dtype=jnp.int32)
    hadamard = parity_sign(positions[:, None] & positions[None, :])

    def whole(shape):
        return pl.BlockSpec(shape, lambda b, *_: (0,) * len(shape), pipeline_mode=pl.Buffered(1))
    step_rows = math.gcd(slab_rows, 4)
    block_specs = [
        pl.BlockSpec((step_rows, slots, order, order), lambda b, *_: (b, 0, 0, 0))
        for _ in range(shares)
    ]
    row_spec = pl.BlockSpec((step_rows * order, half), lambda b, *_: (b, 0))
    flops = 2 * slab_rows * entries * order * order * half
    product = pl.pallas_call(
        functools.partial(inside_kernel, shares, slots, order),
        grid_spec=pltpu.PrefetchScalarGridSpec(
            num_scalar_prefetch=4,
            grid=(slab_rows // step_rows,),
            in_specs=block_specs + [
                pl.BlockSpec((slab_total, half), lambda b, *s: (0, s[3][0]), pipeline_mode=pl.Buffered(1))
            ],
            out_specs=row_spec,
            scratch_shapes=[pltpu.VMEM((slab_rows, order, half), jnp.bfloat16)] * 2,
        ),
        out_shape=jax.ShapeDtypeStruct((slab_total, half), jnp.float32),
        cost_estimate=pl.CostEstimate(flops=6 * flops, bytes_accessed=20 << 20, transcendentals=0),
        name="inside",
    )(which, columns, near, narrow_me.astype(jnp.int32).reshape(1), *all_blocks, vectors)
    gathered, product = lax.optimization_barrier((gathered, product))
    while reach < wide_count:
        gathered, reach = widen(gathered, reach)
    slabs = jnp.arange(wide_count, dtype=jnp.int32)
    rows = jnp.take(gathered, slabs ^ me, axis=0).reshape(samples) % slab_total
    row_signs = parity_sign(slabs & me)
    partial = pl.pallas_call(
        functools.partial(sketch_kernel, shares, slots, order),
        grid_spec=pltpu.PrefetchScalarGridSpec(
            num_scalar_prefetch=5,
            grid=(slab_rows // step_rows,),
            in_specs=block_specs + [
                whole((reach_rows, half)),
                whole((reach_rows, half)),
                row_spec,
                whole((slab_rows, 1, order)),
                whole((order, order)),
            ],
            out_specs=pl.BlockSpec((samples, half), lambda b, *_: (0, 0)),
            scratch_shapes=[
                pltpu.VMEM((2 * REACH, order, half), jnp.bfloat16),
                pltpu.VMEM((2 * REACH, order, half), jnp.bfloat16),
                pltpu.VMEM((order, half), jnp.float32),
                pltpu.VMEM((slab_total, half), jnp.float32),
            ],
        ),
        out_shape=jax.ShapeDtypeStruct((samples, half), jnp.float32),
        cost_estimate=pl.CostEstimate(flops=2 * flops, bytes_accessed=20 << 20, transcendentals=0),
        name="sketch",
    )(which, columns, near, rows, row_signs, *all_blocks, before, after, product,
      sign_bits.reshape(slab_rows, 1, order), hadamard)

    scale = math.sqrt(slab_total * wide_count / samples) / math.sqrt(order * wide_count)
    near_count = 1 << ((wide_count.bit_length() - 1) // 2)
    far_count = wide_count // near_count
    return pl.pallas_call(
        functools.partial(scatter_kernel, scale),
        in_specs=[pl.BlockSpec(memory_space=pltpu.VMEM)],
        out_specs=pl.BlockSpec(memory_space=pltpu.VMEM),
        out_shape=jax.ShapeDtypeStruct((samples_slab, half), jnp.float32),
        scratch_shapes=[
            pltpu.VMEM((near_count, far_count, samples_slab, half), jnp.float32),
            pltpu.VMEM((far_count, samples_slab, half), jnp.float32),
            pltpu.VMEM((far_count, samples_slab, half), jnp.float32),
            pltpu.SemaphoreType.DMA((near_count,)),
            pltpu.SemaphoreType.DMA((near_count,)),
            pltpu.SemaphoreType.DMA((far_count,)),
            pltpu.SemaphoreType.DMA((far_count,)),
        ],
        compiler_params=pltpu.CompilerParams(has_side_effects=True),
        name="scatter",
    )(partial.reshape(far_count, near_count, samples_slab, half))


def solution(mesh):
    return jax.shard_map(
        local,
        mesh=mesh,
        in_specs=(
            P("wide", "narrow", None, None),
            P("wide", None),
            P("wide"),
            P("wide", "narrow"),
            P("wide"),
        ),
        out_specs=P("wide", "narrow"),
        check_vma=False,
    )
```

time: 114 us -> 109 us (0.956)
  the two profiles are of different devices: /device:TPU:14 before, /device:TPU:0 now
where the time goes in v2:
time: 109 us; the launch traced here: 108 us
  Pallas kernels  74.8 us (69%)
  starting transfers between devices  14.9 us (14%)
  waiting for transfers between devices  9.3 us (9%)
  local copies, waits for them, and re-layouts  5.47 us (5%)
  other arithmetic  3.8 us (3%)
    pallas_call x1, Pallas kernels, local(): pl.pallas_call(functools.partial(scatter_kernel, scale), in_specs=[pl.Blo...  28.6 us
    pallas_call x1, Pallas kernels, local(): pl.pallas_call(functools.partial(inside_kernel, shares, slots, order), gr...  25.5 us
    pallas_call x1, Pallas kernels, local(): pl.pallas_call(functools.partial(sketch_kernel, shares, slots, order), gr...  20.7 us
    ppermute x6, starting transfers between devices, widen(): parts.append(lax.ppermute(gathered, 'wide', pairs))  8.52 us
    ppermute x1, waiting for transfers between devices, local(): before = lax.ppermute(last_rows, 'wide', up)  7.51 us
    ppermute x1, starting transfers between devices, local(): after = lax.ppermute(first_rows, 'wide', down)  5.88 us
  transfers between devices with their start and end apart: 10, of which 3 were waited for; matrix products, arithmetic and copies ran while one was open for 7% of the time, Pallas kernels for 24%

profile of v2, /device:TPU:0, one launch (start us, length us, event | category | flops | bytes accessed | tf_op | source)
XLA Modules:
  0.0 108.4 jit_solution(2523150280455481967)
XLA Ops:
  0.0 0.0 copy-start.2
  0.0 0.5 collective-permute-start.4
  0.5 3.5 %collective-permute-start.3 = (s32[1,64]{1,0:T(1,128)}, s32[1,64]{1,0:T(1,128)S(1)}, u32[]{:S(2)}, u32[]{:S(2)}) collective-permute-start(s32[1,64]{1,0:T(1,128)} %bitcast.8), channel_id=1, source_target_pairs={{0,6},{2,4},{4,2},{6,0},{8,14},{10,12},{12,10},{14,8},{16,22},{18,... | collective-permute-start | bytes 776 | tf_op jit(solution)/shard_map/ppermute | solution.py:188
  4.0 0.5 collective-permute-start.2
  4.5 0.1 collective-permute-start.1
  4.6 0.7 add_select_fusion.2
  5.3 0.0 collective-permute-start
  5.4 0.6 subtract_convert_fusion.refs_6_
  6.0 1.7 %constant_dynamic-slice_fusion.1 = (f32[1024,256]{1,0:T(8,128)S(1)}, f32[1024,256]{1,0:T(8,128)S(1)}) fusion(f32[2048,512]{1,0:T(8,128)} %refs_2_.1, s32[]{:T(128)S(6)} %select_n.56), kind=kLoop, calls=%fused_computation.33 | loop fusion | bytes 4194308 | tf_op jit(solution)/shard_map/dynamic_slice | solution.py:198
  7.7 0.6 subtract_convert_fusion.1.row_signs
  8.3 0.0 collective-permute-done.3
  8.3 5.9 %collective-permute-start.9 = (f32[1024,256]{1,0:T(8,128)S(1)}, f32[1024,256]{1,0:T(8,128)S(1)}, u32[]{:S(2)}, u32[]{:S(2)}) collective-permute-start(f32[1024,256]{1,0:T(8,128)S(1)} %get-tuple-element.15), channel_id=1, source_target_pairs={{2,0},{4,2},{6,4},{8,6},{10,8},{12,10},{14,12},{16,14},{18,16},{20... | collective-permute-start | bytes 3145736 | tf_op jit(solution)/shard_map/ppermute | solution.py:200
  14.2 0.0 collective-permute-done.2
  14.2 0.0 collective-permute-start.8
  14.2 0.0 collective-permute-done.1
  14.2 0.0 copy-done.2
  14.2 0.0 collective-permute-done
  14.3 0.0 copy-start.1
  14.3 0.1 copy.13
  14.4 0.1 copy.11
  14.4 0.1 copy.10
  14.5 0.5 multiply_reduce_fusion
  15.1 0.1 copy.12
  15.2 0.5 select_reduce_fusion
  15.7 0.7 copy.17.columns
  16.4 0.7 copy.16.which
  17.1 0.0 collective-permute-done.4.refs_1_
  17.1 0.0 copy-done.1
  17.1 25.5 %inside.1.refs_4_ = f32[2048,256]{1,0:T(8,128)} custom-call(s32[16,14]{1,0:T(8,128)} %copy.16.which, s32[16,14]{1,0:T(8,128)} %copy.17.columns, s32[16]{0:T(128)} %copy-done.1, s32[1]{0:T(128)} %bitcast.1.place, f32[16,7,128,128]{3,2,1,0:T(8,128)} %refs_0_.3, f32[16,7,128,128]{3,2,1,0:T(8,128)} %collective-permute-done.4.refs_1_, f32[2048,512]{1,0:T(8,128)} %refs_2_.1), custom_call_target="tpu_custom_call" | custom-call | flops 11274289152 | bytes 20971520 | tf_op jit(solution)/shard_map/inside/pallas_call | solution.py:236
  42.6 1.7 %collective-permute-start.7 = (s32[4,64]{1,0:T(4,128)S(1)}, s32[4,64]{1,0:T(4,128)S(1)}, u32[]{:S(2)}, u32[]{:S(2)}) collective-permute-start(s32[4,64]{1,0:T(4,128)S(1)} %pad_add_fusion.2), channel_id=1, source_target_pairs={{0,24},{2,26},{4,28},{6,30},{8,16},{10,18},{12,20},{14,22},{16,8},... | collective-permute-start | bytes 3080 | tf_op jit(solution)/shard_map/ppermute | solution.py:188
  44.3 0.0 collective-permute-start.6
  44.3 2.7 %collective-permute-start.5 = (s32[4,64]{1,0:T(4,128)S(1)}, s32[4,64]{1,0:T(4,128)S(1)}, u32[]{:S(2)}, u32[]{:S(2)}) collective-permute-start(s32[4,64]{1,0:T(4,128)S(1)} %pad_add_fusion.2), channel_id=1, source_target_pairs={{0,8},{2,10},{4,12},{6,14},{8,0},{10,2},{12,4},{14,6},{16,24},{18,... | collective-permute-start | bytes 3080 | tf_op jit(solution)/shard_map/ppermute | solution.py:188
  47.0 1.0 collective-permute-done.7
  48.0 0.8 collective-permute-done.6
  48.8 0.0 collective-permute-done.5
  48.8 0.6 gather_fusion
  49.3 0.1 broadcast_select_fusion
  49.4 0.1 select_n.54
  49.5 0.6 add_select_fusion.1.rows
  50.1 0.0 collective-permute-done.9.refs_3_
  50.1 0.0 copy-start
  50.1 7.5 %collective-permute-done.8.refs_2_ = f32[1024,256]{1,0:T(8,128)} collective-permute-done((f32[1024,256]{1,0:T(8,128)S(1)}, f32[1024,256]{1,0:T(8,128)}, u32[]{:S(2)}, u32[]{:S(2)}) %collective-permute-start.8) | collective-permute-done | bytes 1048608 | tf_op jit(solution)/shard_map/ppermute | solution.py:199
  57.6 0.0 copy-done
  57.6 20.7 %sketch.1 = f32[1024,256]{1,0:T(8,128)} custom-call(s32[16,14]{1,0:T(8,128)} %copy.16.which, s32[16,14]{1,0:T(8,128)} %copy.17.columns, s32[16]{0:T(128)} %copy-done.1, s32[1024]{0:T(1024)} %add_select_fusion.1.rows, f32[16]{0:T(128)} %subtract_convert_fusion.1.row_signs, f32[16,7,128,128]{3,2,1,0:T(8,128)} %refs_0_.3, ...), custom_call_target="tpu_custom_call" | custom-call | flops 3758096384 | bytes 20971520 | tf_op jit(solution)/shard_map/sketch/pallas_call | solution.py:257
  78.3 28.6 %scatter.1 = f32[64,256]{1,0:T(8,128)} custom-call(f32[4,4,64,256]{3,2,1,0:T(8,128)} %bitcast.6), custom_call_target="tpu_custom_call" | custom-call | tf_op jit(solution)/shard_map/scatter/pallas_call | solution.py:286
  106.9 1.5 %copy.19 = f32[64,256]{1,0:T(8,128)} copy(f32[64,256]{1,0:T(8,128)} %scatter.1) | data formatting | bytes 131072
  (10 shorter events, 0.1 us)
Async XLA Ops:
  0.0 14.2 %copy-start.2 = (s32[64]{0:T(128)S(1)}, s32[64]{0:T(128)}, u32[]{:S(2)}) copy-start(s32[64]{0:T(128)} %param.9) | copy-start | bytes 772
  0.0 17.1 %collective-permute-start.4 = (f32[16,7,128,128]{3,2,1,0:T(8,128)}, f32[16,7,128,128]{3,2,1,0:T(8,128)}, u32[]{:S(2)}, u32[]{:S(2)}) collective-permute-start(f32[16,7,128,128]{3,2,1,0:T(8,128)} %refs_0_.3), channel_id=1, source_target_pairs={{0,1},{1,0},{2,3},{3,2},{4,5},{5,4},{6,7},{7,6},{8,9},{9,8},{10,11... | collective-permute-start | bytes 22020104 | tf_op jit(solution)/shard_map/ppermute | solution.py:206
  0.5 7.8 %collective-permute-start.3 = (s32[1,64]{1,0:T(1,128)}, s32[1,64]{1,0:T(1,128)S(1)}, u32[]{:S(2)}, u32[]{:S(2)}) collective-permute-start(s32[1,64]{1,0:T(1,128)} %bitcast.8), channel_id=1, source_target_pairs={{0,6},{2,4},{4,2},{6,0},{8,14},{10,12},{12,10},{14,8},{16,22},{18,... | collective-permute-start | bytes 776 | tf_op jit(solution)/shard_map/ppermute | solution.py:188
  4.0 10.2 %collective-permute-start.2 = (s32[1,64]{1,0:T(1,128)}, s32[1,64]{1,0:T(1,128)S(1)}, u32[]{:S(2)}, u32[]{:S(2)}) collective-permute-start(s32[1,64]{1,0:T(1,128)} %bitcast.9), channel_id=1, source_target_pairs={{0,4},{2,6},{4,0},{6,2},{8,12},{10,14},{12,8},{14,10},{16,20},{18,... | collective-permute-start | bytes 776 | tf_op jit(solution)/shard_map/ppermute | solution.py:188
  4.5 9.7 %collective-permute-start.1 = (s32[1,64]{1,0:T(1,128)}, s32[1,64]{1,0:T(1,128)S(1)}, u32[]{:S(2)}, u32[]{:S(2)}) collective-permute-start(s32[1,64]{1,0:T(1,128)} %bitcast.10), channel_id=1, source_target_pairs={{0,2},{2,0},{4,6},{6,4},{8,10},{10,8},{12,14},{14,12},{16,18},{18,... | collective-permute-start | bytes 776 | tf_op jit(solution)/shard_map/ppermute | solution.py:188
  5.3 8.9 %collective-permute-start = (s32[16,7]{0,1:T(8,128)S(1)}, s32[16,7]{0,1:T(8,128)S(1)}, u32[]{:S(2)}, u32[]{:S(2)}) collective-permute-start(s32[16,7]{0,1:T(8,128)S(1)} %add_select_fusion.2), channel_id=1, source_target_pairs={{0,1},{1,0},{2,3},{3,2},{4,5},{5,4},{6,7},{7,6},{8,9},{9,8},{10,11... | collective-permute-start | bytes 1352 | tf_op jit(solution)/shard_map/ppermute | solution.py:207
  8.3 41.8 %collective-permute-start.9 = (f32[1024,256]{1,0:T(8,128)S(1)}, f32[1024,256]{1,0:T(8,128)S(1)}, u32[]{:S(2)}, u32[]{:S(2)}) collective-permute-start(f32[1024,256]{1,0:T(8,128)S(1)} %get-tuple-element.15), channel_id=1, source_target_pairs={{2,0},{4,2},{6,4},{8,6},{10,8},{12,10},{14,12},{16,14},{18,16},{20... | collective-permute-start | bytes 3145736 | tf_op jit(solution)/shard_map/ppermute | solution.py:200
  14.2 43.4 %collective-permute-start.8 = (f32[1024,256]{1,0:T(8,128)S(1)}, f32[1024,256]{1,0:T(8,128)}, u32[]{:S(2)}, u32[]{:S(2)}) collective-permute-start(f32[1024,256]{1,0:T(8,128)S(1)} %get-tuple-element.16), channel_id=1, source_target_pairs={{0,2},{2,4},{4,6},{6,8},{8,10},{10,12},{12,14},{14,16},{16,18},{18... | collective-permute-start | bytes 3145736 | tf_op jit(solution)/shard_map/ppermute | solution.py:199
  14.3 2.8 %copy-start.1 = (s32[16]{0:T(128)}, s32[16]{0:T(128)S(1)}, u32[]{:S(2)}) copy-start(s32[16]{0:T(128)S(1)} %get-tuple-element.13.near) | copy-start | bytes 196
  42.6 5.4 %collective-permute-start.7 = (s32[4,64]{1,0:T(4,128)S(1)}, s32[4,64]{1,0:T(4,128)S(1)}, u32[]{:S(2)}, u32[]{:S(2)}) collective-permute-start(s32[4,64]{1,0:T(4,128)S(1)} %pad_add_fusion.2), channel_id=1, source_target_pairs={{0,24},{2,26},{4,28},{6,30},{8,16},{10,18},{12,20},{14,22},{16,8},... | collective-permute-start | bytes 3080 | tf_op jit(solution)/shard_map/ppermute | solution.py:188
  44.3 4.5 %collective-permute-start.6 = (s32[4,64]{1,0:T(4,128)S(1)}, s32[4,64]{1,0:T(4,128)S(1)}, u32[]{:S(2)}, u32[]{:S(2)}) collective-permute-start(s32[4,64]{1,0:T(4,128)S(1)} %pad_add_fusion.2), channel_id=1, source_target_pairs={{0,16},{2,18},{4,20},{6,22},{8,24},{10,26},{12,28},{14,30},{16,0},... | collective-permute-start | bytes 3080 | tf_op jit(solution)/shard_map/ppermute | solution.py:188
  44.3 4.5 %collective-permute-start.5 = (s32[4,64]{1,0:T(4,128)S(1)}, s32[4,64]{1,0:T(4,128)S(1)}, u32[]{:S(2)}, u32[]{:S(2)}) collective-permute-start(s32[4,64]{1,0:T(4,128)S(1)} %pad_add_fusion.2), channel_id=1, source_target_pairs={{0,8},{2,10},{4,12},{6,14},{8,0},{10,2},{12,4},{14,6},{16,24},{18,... | collective-permute-start | bytes 3080 | tf_op jit(solution)/shard_map/ppermute | solution.py:188
  50.1 7.5 %copy-start = (f32[1024,256]{1,0:T(8,128)}, f32[1024,256]{1,0:T(8,128)S(1)}, u32[]{:S(2)}) copy-start(f32[1024,256]{1,0:T(8,128)S(1)} %collective-permute-done.9.refs_3_) | copy-start | bytes 3145732

commit v3 on v2

--- a/solution.py
+++ b/solution.py
@@ -25,22 +25,28 @@
             found = jnp.where(which_at // slots == share, blocks[share][r, which_at % slots], found)
         return found
 
-    def pair(i, carry):
-        one = first + 2 * i
-        two = jnp.minimum(one + 1, last - 1)
-        kept = (one + 1 < last).astype(jnp.float32)
-        a = jnp.concatenate([block(one), block(two) * kept], axis=1)
-        a_high, a_low = split_bf16(a)
-        where = [shift(columns[b, at]) for at in (one, two)]
-        v_high = jnp.concatenate([high[w] for w in where], axis=0)
-        v_low = jnp.concatenate([low[w] for w in where], axis=0)
-        both = jnp.dot(
-            jnp.concatenate([a_high, a_low], axis=0), v_high, preferred_element_type=jnp.float32
-        )
-        small = jnp.dot(a_high, v_low, preferred_element_type=jnp.float32)
-        total[...] += both[:order] + (both[order:] + small)
-        return carry
-    lax.fori_loop(0, (last - first + 1) // 2, pair, 0)
+    group = 4
+
+    def several(i, carry):
+        parts = []
+        for at in range(0, group, 2):
+            entries = [first + group * i + at + k for k in range(2)]
+            found = [jnp.minimum(e, last - 1) for e in entries]
+            a = jnp.concatenate(
+                [block(f) * (e < last).astype(jnp.float32) for e, f in zip(entries, found)], axis=1
+            )
+            a_high, a_low = split_bf16(a)
+            where = [shift(columns[b, f]) for f in found]
+            v_high = jnp.concatenate([high[w] for w in where], axis=0)
+            v_low = jnp.concatenate([low[w] for w in where], axis=0)
+            both = jnp.dot(
+                jnp.concatenate([a_high, a_low], axis=0), v_high, preferred_element_type=jnp.float32
+            )
+            small = jnp.dot(a_high, v_low, preferred_element_type=jnp.float32)
+            parts.append(both[:order] + (both[order:] + small))
+        total[...] += functools.reduce(jnp.add, parts)
+        return carry
+    lax.fori_loop(0, (last - first + group - 1) // group, several, 0)
 
 
 def convert_rows(piece, start, order, high, low):

time: 109 us -> 107 us (0.982)
  Pallas kernels: 74.8 us -> 65.7 us
  waiting for transfers between devices: 9.3 us -> 15.9 us
    pallas_call x1, Pallas kernels: 25.5 us -> 19 us  [local(): pl.pallas_call(functools.partial(inside_kernel, shares, slots, order), gr...]
    ppermute x1, waiting for transfers between devices: 7.51 us -> 13.5 us  [local(): before = lax.ppermute(last_rows, 'wide', up)]
    pallas_call x1, Pallas kernels: 20.7 us -> 17.7 us  [local(): pl.pallas_call(functools.partial(sketch_kernel, shares, slots, order), gr...]
  transfers between devices with their start and end apart: 10 -> 10, of which waited for: 3 -> 3; matrix products, arithmetic and copies ran while one was open for 7% -> 7% of each run, Pallas kernels for 24% -> 18%
where the time goes in v3:
time: 107 us; the launch traced here: 106 us
  Pallas kernels  65.7 us (61%)
  waiting for transfers between devices  15.9 us (15%)
  starting transfers between devices  14.9 us (14%)
  local copies, waits for them, and re-layouts  5.47 us (5%)
  other arithmetic  3.8 us (4%)
    pallas_call x1, Pallas kernels, local(): pl.pallas_call(functools.partial(scatter_kernel, scale), in_specs=[pl.Blo...  29.1 us
    pallas_call x1, Pallas kernels, local(): pl.pallas_call(functools.partial(inside_kernel, shares, slots, order), gr...  19 us
    pallas_call x1, Pallas kernels, local(): pl.pallas_call(functools.partial(sketch_kernel, shares, slots, order), gr...  17.7 us
    ppermute x1, waiting for transfers between devices, local(): before = lax.ppermute(last_rows, 'wide', up)  13.5 us
    ppermute x6, starting transfers between devices, widen(): parts.append(lax.ppermute(gathered, 'wide', pairs))  8.52 us
    ppermute x1, starting transfers between devices, local(): after = lax.ppermute(first_rows, 'wide', down)  5.88 us
    ppermute x6, waiting for transfers between devices, widen(): parts.append(lax.ppermute(gathered, 'wide', pairs))  2.38 us
  transfers between devices with their start and end apart: 10, of which 3 were waited for; matrix products, arithmetic and copies ran while one was open for 7% of the time, Pallas kernels for 18%

profile of v3, /device:TPU:0, one launch (start us, length us, event | category | flops | bytes accessed | tf_op | source)
XLA Modules:
  0.0 105.9 jit_solution(265526799365850012)
XLA Ops:
  0.0 0.0 copy-start.2
  0.0 0.5 collective-permute-start.4
  0.5 3.5 %collective-permute-start.3 = (s32[1,64]{1,0:T(1,128)}, s32[1,64]{1,0:T(1,128)S(1)}, u32[]{:S(2)}, u32[]{:S(2)}) collective-permute-start(s32[1,64]{1,0:T(1,128)} %bitcast.8), channel_id=1, source_target_pairs={{0,6},{2,4},{4,2},{6,0},{8,14},{10,12},{12,10},{14,8},{16,22},{18,... | collective-permute-start | bytes 776 | tf_op jit(solution)/shard_map/ppermute | solution.py:194
  4.0 0.5 collective-permute-start.2
  4.5 0.1 collective-permute-start.1
  4.6 0.7 add_select_fusion.2
  5.3 0.0 collective-permute-start
  5.4 0.6 subtract_convert_fusion.refs_6_
  6.0 1.7 %constant_dynamic-slice_fusion.1 = (f32[1024,256]{1,0:T(8,128)S(1)}, f32[1024,256]{1,0:T(8,128)S(1)}) fusion(f32[2048,512]{1,0:T(8,128)} %refs_2_.1, s32[]{:T(128)S(6)} %select_n.56), kind=kLoop, calls=%fused_computation.33 | loop fusion | bytes 4194308 | tf_op jit(solution)/shard_map/dynamic_slice | solution.py:204
  7.7 0.6 subtract_convert_fusion.1.row_signs
  8.3 0.0 collective-permute-done.3
  8.3 5.9 %collective-permute-start.9 = (f32[1024,256]{1,0:T(8,128)S(1)}, f32[1024,256]{1,0:T(8,128)S(1)}, u32[]{:S(2)}, u32[]{:S(2)}) collective-permute-start(f32[1024,256]{1,0:T(8,128)S(1)} %get-tuple-element.15), channel_id=1, source_target_pairs={{2,0},{4,2},{6,4},{8,6},{10,8},{12,10},{14,12},{16,14},{18,16},{20... | collective-permute-start | bytes 3145736 | tf_op jit(solution)/shard_map/ppermute | solution.py:206
  14.2 0.0 collective-permute-done.2
  14.2 0.0 collective-permute-start.8
  14.2 0.0 collective-permute-done.1
  14.2 0.0 copy-done.2
  14.2 0.0 collective-permute-done
  14.3 0.0 copy-start.1
  14.3 0.1 copy.13
  14.4 0.1 copy.11
  14.4 0.1 copy.10
  14.5 0.5 multiply_reduce_fusion
  15.1 0.1 copy.12
  15.2 0.5 select_reduce_fusion
  15.7 0.7 copy.17.columns
  16.4 0.7 copy.16.which
  17.1 0.0 collective-permute-done.4.refs_1_
  17.1 0.0 copy-done.1
  17.1 19.0 %inside.1.refs_4_ = f32[2048,256]{1,0:T(8,128)} custom-call(s32[16,14]{1,0:T(8,128)} %copy.16.which, s32[16,14]{1,0:T(8,128)} %copy.17.columns, s32[16]{0:T(128)} %copy-done.1, s32[1]{0:T(128)} %bitcast.1.place, f32[16,7,128,128]{3,2,1,0:T(8,128)} %refs_0_.3, f32[16,7,128,128]{3,2,1,0:T(8,128)} %collective-permute-done.4.refs_1_, f32[2048,512]{1,0:T(8,128)} %refs_2_.1), custom_call_target="tpu_custom_call" | custom-call | flops 11274289152 | bytes 20971520 | tf_op jit(solution)/shard_map/inside/pallas_call | solution.py:242
  36.0 2.3 %collective-permute-start.7 = (s32[4,64]{1,0:T(4,128)S(1)}, s32[4,64]{1,0:T(4,128)S(1)}, u32[]{:S(2)}, u32[]{:S(2)}) collective-permute-start(s32[4,64]{1,0:T(4,128)S(1)} %pad_add_fusion.2), channel_id=1, source_target_pairs={{0,24},{2,26},{4,28},{6,30},{8,16},{10,18},{12,20},{14,22},{16,8},... | collective-permute-start | bytes 3080 | tf_op jit(solution)/shard_map/ppermute | solution.py:194
  38.3 0.1 collective-permute-start.6
  38.4 2.0 %collective-permute-start.5 = (s32[4,64]{1,0:T(4,128)S(1)}, s32[4,64]{1,0:T(4,128)S(1)}, u32[]{:S(2)}, u32[]{:S(2)}) collective-permute-start(s32[4,64]{1,0:T(4,128)S(1)} %pad_add_fusion.2), channel_id=1, source_target_pairs={{0,8},{2,10},{4,12},{6,14},{8,0},{10,2},{12,4},{14,6},{16,24},{18,... | collective-permute-start | bytes 3080 | tf_op jit(solution)/shard_map/ppermute | solution.py:194
  40.4 1.0 collective-permute-done.7
  41.4 1.4 %collective-permute-done.6 = s32[4,64]{1,0:T(4,128)S(1)} collective-permute-done((s32[4,64]{1,0:T(4,128)S(1)}, s32[4,64]{1,0:T(4,128)S(1)}, u32[]{:S(2)}, u32[]{:S(2)}) %collective-permute-start.6) | collective-permute-done | bytes 1056 | tf_op jit(solution)/shard_map/ppermute | solution.py:194
  42.8 0.0 collective-permute-done.5
  42.8 0.6 gather_fusion
  43.4 0.1 broadcast_select_fusion
  43.5 0.1 select_n.54
  43.5 0.6 add_select_fusion.1.rows
  44.1 0.0 collective-permute-done.9.refs_3_
  44.1 0.0 copy-start
  44.2 13.5 %collective-permute-done.8.refs_2_ = f32[1024,256]{1,0:T(8,128)} collective-permute-done((f32[1024,256]{1,0:T(8,128)S(1)}, f32[1024,256]{1,0:T(8,128)}, u32[]{:S(2)}, u32[]{:S(2)}) %collective-permute-start.8) | collective-permute-done | bytes 1048608 | tf_op jit(solution)/shard_map/ppermute | solution.py:205
  57.6 0.0 copy-done
  57.6 17.7 %sketch.1 = f32[1024,256]{1,0:T(8,128)} custom-call(s32[16,14]{1,0:T(8,128)} %copy.16.which, s32[16,14]{1,0:T(8,128)} %copy.17.columns, s32[16]{0:T(128)} %copy-done.1, s32[1024]{0:T(1024)} %add_select_fusion.1.rows, f32[16]{0:T(128)} %subtract_convert_fusion.1.row_signs, f32[16,7,128,128]{3,2,1,0:T(8,128)} %refs_0_.3, ...), custom_call_target="tpu_custom_call" | custom-call | flops 3758096384 | bytes 20971520 | tf_op jit(solution)/shard_map/sketch/pallas_call | solution.py:263
  75.3 29.1 %scatter.1 = f32[64,256]{1,0:T(8,128)} custom-call(f32[4,4,64,256]{3,2,1,0:T(8,128)} %bitcast.6), custom_call_target="tpu_custom_call" | custom-call | tf_op jit(solution)/shard_map/scatter/pallas_call | solution.py:292
  104.4 1.5 %copy.19 = f32[64,256]{1,0:T(8,128)} copy(f32[64,256]{1,0:T(8,128)} %scatter.1) | data formatting | bytes 131072
  (10 shorter events, 0.1 us)
Async XLA Ops:
  0.0 14.2 %copy-start.2 = (s32[64]{0:T(128)S(1)}, s32[64]{0:T(128)}, u32[]{:S(2)}) copy-start(s32[64]{0:T(128)} %param.9) | copy-start | bytes 772
  0.0 17.1 %collective-permute-start.4 = (f32[16,7,128,128]{3,2,1,0:T(8,128)}, f32[16,7,128,128]{3,2,1,0:T(8,128)}, u32[]{:S(2)}, u32[]{:S(2)}) collective-permute-start(f32[16,7,128,128]{3,2,1,0:T(8,128)} %refs_0_.3), channel_id=1, source_target_pairs={{0,1},{1,0},{2,3},{3,2},{4,5},{5,4},{6,7},{7,6},{8,9},{9,8},{10,11... | collective-permute-start | bytes 22020104 | tf_op jit(solution)/shard_map/ppermute | solution.py:212
  0.5 7.8 %collective-permute-start.3 = (s32[1,64]{1,0:T(1,128)}, s32[1,64]{1,0:T(1,128)S(1)}, u32[]{:S(2)}, u32[]{:S(2)}) collective-permute-start(s32[1,64]{1,0:T(1,128)} %bitcast.8), channel_id=1, source_target_pairs={{0,6},{2,4},{4,2},{6,0},{8,14},{10,12},{12,10},{14,8},{16,22},{18,... | collective-permute-start | bytes 776 | tf_op jit(solution)/shard_map/ppermute | solution.py:194
  4.0 10.2 %collective-permute-start.2 = (s32[1,64]{1,0:T(1,128)}, s32[1,64]{1,0:T(1,128)S(1)}, u32[]{:S(2)}, u32[]{:S(2)}) collective-permute-start(s32[1,64]{1,0:T(1,128)} %bitcast.9), channel_id=1, source_target_pairs={{0,4},{2,6},{4,0},{6,2},{8,12},{10,14},{12,8},{14,10},{16,20},{18,... | collective-permute-start | bytes 776 | tf_op jit(solution)/shard_map/ppermute | solution.py:194
  4.5 9.7 %collective-permute-start.1 = (s32[1,64]{1,0:T(1,128)}, s32[1,64]{1,0:T(1,128)S(1)}, u32[]{:S(2)}, u32[]{:S(2)}) collective-permute-start(s32[1,64]{1,0:T(1,128)} %bitcast.10), channel_id=1, source_target_pairs={{0,2},{2,0},{4,6},{6,4},{8,10},{10,8},{12,14},{14,12},{16,18},{18,... | collective-permute-start | bytes 776 | tf_op jit(solution)/shard_map/ppermute | solution.py:194
  5.3 8.9 %collective-permute-start = (s32[16,7]{0,1:T(8,128)S(1)}, s32[16,7]{0,1:T(8,128)S(1)}, u32[]{:S(2)}, u32[]{:S(2)}) collective-permute-start(s32[16,7]{0,1:T(8,128)S(1)} %add_select_fusion.2), channel_id=1, source_target_pairs={{0,1},{1,0},{2,3},{3,2},{4,5},{5,4},{6,7},{7,6},{8,9},{9,8},{10,11... | collective-permute-start | bytes 1352 | tf_op jit(solution)/shard_map/ppermute | solution.py:213
  8.3 35.9 %collective-permute-start.9 = (f32[1024,256]{1,0:T(8,128)S(1)}, f32[1024,256]{1,0:T(8,128)S(1)}, u32[]{:S(2)}, u32[]{:S(2)}) collective-permute-start(f32[1024,256]{1,0:T(8,128)S(1)} %get-tuple-element.15), channel_id=1, source_target_pairs={{2,0},{4,2},{6,4},{8,6},{10,8},{12,10},{14,12},{16,14},{18,16},{20... | collective-permute-start | bytes 3145736 | tf_op jit(solution)/shard_map/ppermute | solution.py:206
  14.2 43.4 %collective-permute-start.8 = (f32[1024,256]{1,0:T(8,128)S(1)}, f32[1024,256]{1,0:T(8,128)}, u32[]{:S(2)}, u32[]{:S(2)}) collective-permute-start(f32[1024,256]{1,0:T(8,128)S(1)} %get-tuple-element.16), channel_id=1, source_target_pairs={{0,2},{2,4},{4,6},{6,8},{8,10},{10,12},{12,14},{14,16},{16,18},{18... | collective-permute-start | bytes 3145736 | tf_op jit(solution)/shard_map/ppermute | solution.py:205
  14.3 2.8 %copy-start.1 = (s32[16]{0:T(128)}, s32[16]{0:T(128)S(1)}, u32[]{:S(2)}) copy-start(s32[16]{0:T(128)S(1)} %get-tuple-element.13.near) | copy-start | bytes 196
  36.0 5.4 %collective-permute-start.7 = (s32[4,64]{1,0:T(4,128)S(1)}, s32[4,64]{1,0:T(4,128)S(1)}, u32[]{:S(2)}, u32[]{:S(2)}) collective-permute-start(s32[4,64]{1,0:T(4,128)S(1)} %pad_add_fusion.2), channel_id=1, source_target_pairs={{0,24},{2,26},{4,28},{6,30},{8,16},{10,18},{12,20},{14,22},{16,8},... | collective-permute-start | bytes 3080 | tf_op jit(solution)/shard_map/ppermute | solution.py:194
  38.3 4.5 %collective-permute-start.6 = (s32[4,64]{1,0:T(4,128)S(1)}, s32[4,64]{1,0:T(4,128)S(1)}, u32[]{:S(2)}, u32[]{:S(2)}) collective-permute-start(s32[4,64]{1,0:T(4,128)S(1)} %pad_add_fusion.2), channel_id=1, source_target_pairs={{0,16},{2,18},{4,20},{6,22},{8,24},{10,26},{12,28},{14,30},{16,0},... | collective-permute-start | bytes 3080 | tf_op jit(solution)/shard_map/ppermute | solution.py:194
  38.4 4.4 %collective-permute-start.5 = (s32[4,64]{1,0:T(4,128)S(1)}, s32[4,64]{1,0:T(4,128)S(1)}, u32[]{:S(2)}, u32[]{:S(2)}) collective-permute-start(s32[4,64]{1,0:T(4,128)S(1)} %pad_add_fusion.2), channel_id=1, source_target_pairs={{0,8},{2,10},{4,12},{6,14},{8,0},{10,2},{12,4},{14,6},{16,24},{18,... | collective-permute-start | bytes 3080 | tf_op jit(solution)/shard_map/ppermute | solution.py:194
  44.1 13.5 %copy-start = (f32[1024,256]{1,0:T(8,128)}, f32[1024,256]{1,0:T(8,128)S(1)}, u32[]{:S(2)}) copy-start(f32[1024,256]{1,0:T(8,128)S(1)} %collective-permute-done.9.refs_3_) | copy-start | bytes 3145732
